TPU v7x, 32 devices: a whole 2x2x4 slice. The times are simulated.
32 devices in a mesh: seq: 8 (over z, y), head: 2 (over x), dp: 2 (over core).
Axes of the slice: x: 2, y: 2, z: 4, core: 2. Of those that a mesh axis runs over, the one named last changes fastest.
Arguments:
- queries: bfloat16 [2048, 4096], P(('dp', 'seq'), 'head'), parts along dimension 0, may hold values from -6 to 6
- key_vectors: bfloat16 [2048, 4096], P(('dp', 'seq'), 'head'), parts along dimension 0, may hold values from -6 to 6
- value_vectors: bfloat16 [2048, 4096], P(('dp', 'seq'), 'head'), parts along dimension 0, may hold values from -6 to 6
- grad_out: bfloat16 [2048, 4096], P(('dp', 'seq'), 'head'), parts along dimension 0, may hold values from -6 to 6
Outputs:
- grad_queries: bfloat16 [2048, 4096], P(('dp', 'seq'), 'head'), parts along dimension 0
- grad_keys: bfloat16 [2048, 4096], P(('dp', 'seq'), 'head'), parts along dimension 0
- grad_values: bfloat16 [2048, 4096], P(('dp', 'seq'), 'head'), parts along dimension 0
There are 2 independent parts, one for each index of `dp`. A program takes and returns all parts, laid end to end along the dimension named above; each array names one. Nothing has to cross between parts.
All inputs are finite; a program needn't handle non-finite values.
Results may differ from a plain program's by a relative error of at most 0.012.
Values may be sent and summed in bfloat16 or wider, within the bound.
No kernel may reach another device: no remote copies, remote signals or barrier semaphores. Data moves between devices by JAX's collectives and lax.ppermute only.
A program may use at most 128 MiB of HBM per device.

v0:
```python
import jax
import jax.numpy as jnp
from jax import lax
from jax.sharding import PartitionSpec as P

E = 128
B = 128
masked_value = -1e30


def passed_along(block, axis, distance):
    devices = range(lax.axis_size(axis))
    route = [(i - distance, i) for i in devices if i - distance in devices]
    return lax.ppermute(block, axis, route)


def prefix(part, axis, combine, identity):
    count = lax.axis_size(axis)
    place = lax.axis_index(axis)
    ahead = count - 1 - place
    gathered = jax.tree.map(lambda a: lax.all_gather(a, axis), part)
    state = jax.tree.map(lambda a, e: jnp.zeros_like(a) + jnp.asarray(e, a.dtype), part, identity)

    def one(turn, state):
        source = count - 1 - turn
        return combine(
            state, jax.tree.map(lambda a: lax.dynamic_index_in_dim(a, source, 0, False), gathered)
        )

    return lax.fori_loop(0, ahead, one, state)


def scores(query_part, key_part, allowed):
    scaling = query_part.shape[2] ** (-0.5)
    logits = (
        jnp.einsum("qhe,khe->hqk", query_part, key_part, preferred_element_type=jnp.float32)
        * scaling
    )
    return jnp.where(allowed[None], logits, masked_value)


def backward_terms(query_part, value_part, grad_part, logits, log_total, inner_term):
    scaling = query_part.shape[2] ** (-0.5)
    probs = jnp.exp(logits - log_total)
    probs_low = probs.astype(jnp.bfloat16)
    grad_probs = jnp.einsum(
        "qhe,khe->hqk", grad_part, value_part, preferred_element_type=jnp.float32
    )
    grad_logits = (probs * (grad_probs - inner_term)).astype(jnp.bfloat16)
    grad_keyset = scaling * jnp.einsum(
        "hqk,qhe->khe", grad_logits, query_part, preferred_element_type=jnp.float32
    )
    grad_valset = jnp.einsum(
        "hqk,qhe->khe", probs_low, grad_part, preferred_element_type=jnp.float32
    )
    return (grad_logits, grad_keyset, grad_valset)


def attend_back(query_part, key_part, value_part, grad_part, allowed):
    scaling = query_part.shape[2] ** (-0.5)
    logits = scores(query_part, key_part, allowed)
    row_max = jnp.max(logits, axis=2, keepdims=True)
    log_total = row_max + jnp.log(jnp.sum(jnp.exp(logits - row_max), axis=2, keepdims=True))
    probs_low = jnp.exp(logits - log_total).astype(jnp.bfloat16)
    output = jnp.einsum("hqk,khe->qhe", probs_low, value_part, preferred_element_type=jnp.float32)
    inner_term = jnp.einsum("qhe,qhe->hq", grad_part.astype(jnp.float32), output)[:, :, None]
    grad_logits, grad_keyset, grad_valset = backward_terms(
        query_part, value_part, grad_part, logits, log_total, inner_term
    )
    grad_query = scaling * jnp.einsum(
        "hqk,khe->qhe", grad_logits, key_part, preferred_element_type=jnp.float32
    )
    return (grad_query, grad_keyset, grad_valset, log_total, inner_term)


def add_pair(earlier, later):
    return (earlier[0] + later[0], earlier[1] + later[1])


def body(queries, key_vectors, value_vectors, grad_out):
    shard_len, feature_count = queries.shape
    head_count = feature_count // E
    block_count = shard_len // B
    offset = lax.axis_index("seq") * shard_len
    query_heads = queries.reshape(shard_len, head_count, E)
    key_heads = key_vectors.reshape(shard_len, head_count, E)
    value_heads = value_vectors.reshape(shard_len, head_count, E)
    grad_heads = grad_out.reshape(shard_len, head_count, E)
    halo_key, halo_value = passed_along((key_heads, value_heads), "seq", 1)
    key_blocks = key_heads.reshape(block_count, B, head_count, E)
    value_blocks = value_heads.reshape(block_count, B, head_count, E)
    query_blocks = query_heads.reshape(block_count, B, head_count, E)
    grad_blocks = grad_heads.reshape(block_count, B, head_count, E)
    strided_key = key_blocks[:, B - 1]
    strided_value = value_blocks[:, B - 1]
    summary_key, summary_value = (
        lax.all_gather(strided_key, "seq", axis=0, tiled=True),
        lax.all_gather(strided_value, "seq", axis=0, tiled=True),
    )
    summary_count = summary_key.shape[0]
    key_before = jnp.concatenate([halo_key[None], key_blocks[:-1]], axis=0)
    value_before = jnp.concatenate([halo_value[None], value_blocks[:-1]], axis=0)
    steps_b = jnp.arange(B, dtype=jnp.int32)
    summary_pos = jnp.arange(summary_count, dtype=jnp.int32) * B + B - 1
    is_local = jnp.arange(2 * B + summary_count, dtype=jnp.int32) < 2 * B

    def one_block(local_index, query_part, key_prev, key_here, value_prev, value_here, grad_part):
        block_start = offset + local_index * B
        key_set = jnp.concatenate([key_prev, key_here, summary_key], axis=0)
        value_set = jnp.concatenate([value_prev, value_here, summary_value], axis=0)
        query_pos = block_start + steps_b
        key_pos = jnp.concatenate([block_start - B + steps_b, block_start + steps_b, summary_pos])
        near = (
            (key_pos[None, :] > query_pos[:, None] - B)
            & (key_pos[None, :] <= query_pos[:, None])
            & (key_pos[None, :] >= 0)
        )
        far_ok = key_pos[None, :] <= query_pos[:, None] - B
        allowed = jnp.where(is_local[None, :], near, far_ok)
        return attend_back(query_part, key_set, value_set, grad_part, allowed)

    grad_query, grad_keyset, grad_valset, log_total, inner_term = jax.vmap(one_block)(
        jnp.arange(block_count, dtype=jnp.int32),
        query_blocks,
        key_before,
        key_blocks,
        value_before,
        value_blocks,
        grad_blocks,
    )
    empty_grad = jnp.zeros((1, B, head_count, E), jnp.float32)
    own_key = grad_keyset[:, B : 2 * B] + jnp.concatenate([grad_keyset[1:, :B], empty_grad], axis=0)
    own_value = grad_valset[:, B : 2 * B] + jnp.concatenate(
        [grad_valset[1:, :B], empty_grad], axis=0
    )
    back_key, back_value = (
        passed_along(grad_keyset[0, :B].astype(jnp.bfloat16), "seq", -1).astype(jnp.float32),
        passed_along(grad_valset[0, :B].astype(jnp.bfloat16), "seq", -1).astype(jnp.float32),
    )
    own_key = own_key.at[block_count - 1].add(back_key)
    own_value = own_value.at[block_count - 1].add(back_value)
    summary_gk = jnp.sum(grad_keyset[:, 2 * B :], axis=0)
    summary_gv = jnp.sum(grad_valset[:, 2 * B :], axis=0)
    empty_sum = jnp.zeros_like(summary_gk)
    later_key, later_value = prefix(
        (summary_gk, summary_gv), "seq", add_pair, (empty_sum, empty_sum)
    )
    start_row = lax.axis_index("seq") * block_count
    mine_key = lax.dynamic_slice_in_dim(later_key + summary_gk, start_row, block_count, 0)
    mine_value = lax.dynamic_slice_in_dim(later_value + summary_gv, start_row, block_count, 0)
    own_key = own_key.at[:, B - 1].add(mine_key)
    own_value = own_value.at[:, B - 1].add(mine_value)
    return (
        grad_query.reshape(shard_len, feature_count).astype(jnp.bfloat16),
        own_key.reshape(shard_len, feature_count).astype(jnp.bfloat16),
        own_value.reshape(shard_len, feature_count).astype(jnp.bfloat16),
    )


def solution(mesh):
    return jax.shard_map(
        body,
        mesh=mesh,
        in_specs=(
            P(("dp", "seq"), "head"),
            P(("dp", "seq"), "head"),
            P(("dp", "seq"), "head"),
            P(("dp", "seq"), "head"),
        ),
        out_specs=(P(("dp", "seq"), "head"), P(("dp", "seq"), "head"), P(("dp", "seq"), "head")),
        check_vma=False,
    )
```

profile of v0, /device:TPU:0, one launch (start us, length us, event | category | flops | bytes accessed | tf_op | source)
XLA Modules:
  0.0 187.8 jit_solution(2531822382661108834)
XLA Ops:
  0.7 1.4 copy.41
  2.3 5.7 %collective-permute-start = (bf16[128,16,128]{2,0,1:T(8,128)(2,1)S(1)}, bf16[128,16,128]{2,0,1:T(8,128)(2,1)}, u32[]{:S(2)}, u32[]{:S(2)}) collective-permute-start(bf16[128,16,128]{2,0,1:T(8,128)(2,1)S(1)} %copy.42), channel_id=1, source_target_pairs={{0,4},{4,8},{8,12},{12,16},{16,20},{20,24},{24,28},{1,5},{5,9},{9,... | collective-permute-start | bytes 1572872 | tf_op jit(solution)/shard_map/ppermute | solution.py:14
  8.3 1.0 copy.49
  9.3 3.4 %collective-permute-start.1 = (bf16[128,16,128]{2,0,1:T(8,128)(2,1)}, bf16[128,16,128]{2,0,1:T(8,128)(2,1)}, u32[]{:S(2)}, u32[]{:S(2)}) collective-permute-start(bf16[128,16,128]{2,0,1:T(8,128)(2,1)} %copy.49), channel_id=1, source_target_pairs={{0,4},{4,8},{8,12},{12,16},{16,20},{20,24},{24,28},{1,5},{5,9},{9,... | collective-permute-start | bytes 1572872 | tf_op jit(solution)/shard_map/ppermute | solution.py:14
  13.0 1.0 copy.46
  14.2 1.0 copy.53
  15.4 40.1 %all-gather = bf16[8,1,16,128]{3,2,1,0:T(8,128)(2,1)S(1)} all-gather(bf16[1,1,16,128]{3,2,1,0:T(8,128)(2,1)S(1)} %copy.44), channel_id=2, replica_groups=mesh['seq'=8,'head'=2,'dp'=2] {'seq'}, dimensions={0}, use_global_device_ids=true | all-gather | bytes 36864 | tf_op jit(solution)/shard_map/all_gather | solution.py:97
  55.8 30.4 %all-gather.1 = bf16[8,1,16,128]{3,2,1,0:T(8,128)(2,1)S(1)} all-gather(bf16[1,1,16,128]{3,2,1,0:T(8,128)(2,1)S(1)} %copy.51), channel_id=3, replica_groups=mesh['seq'=8,'head'=2,'dp'=2] {'seq'}, dimensions={0}, use_global_device_ids=true | all-gather | bytes 36864 | tf_op jit(solution)/shard_map/all_gather | solution.py:98
  86.2 0.9 copy.75
  87.4 1.9 %fusion.24 = (f32[16,128]{1,0:T(8,128)S(1)}, f32[16,128,264]{1,2,0:T(8,128)S(1)}) fusion(bf16[1,8,16,128]{3,1,2,0:T(8,128)(2,1)S(1)} %bitcast.126, bf16[1,128,16,128]{3,1,2,0:T(8,128)(2,1)} %copy.46, bf16[1,128,16,128]{3,1,2,0:T(8,128)(2,1)} %bitcast.5, pred[128,264]{0,1:T(8,128)(4,1)S(1)} %compare_select_fusion, bf16[128,2048]{1,0:T(8,128)(2,1)S(1)} %copy-done), kind=kOutput, calls=%fused_computation.55 | convolution fusion | flops 143276032 | bytes 3810304 | tf_op jit(solution)/shard_map/vmap(qhe,khe->hqk)/dot_general | solution.py:36
  89.7 0.7 copy-done.7
  90.4 2.9 %convolution_bitcast_fusion.1 = f32[16,128,128]{1,2,0:T(8,128)} fusion(bf16[1,8,16,128]{3,1,2,0:T(8,128)(2,1)S(1)} %bitcast.128, bf16[1,128,16,128]{3,1,2,0:T(8,128)(2,1)S(1)} %copy-done.7, bf16[1,128,16,128]{3,1,2,0:T(8,128)(2,1)} %bitcast.11, f32[16,128,264]{1,2,0:T(8,128)S(1)} %get-tuple-element.174, f32[16,128]{1,0:T(8,128)S(1)} %log_add_fusion), kind=kOutput, calls=%fused_computation.11 | convolution fusion | flops 142737408 | bytes 4300800 | tf_op jit(solution)/shard_map/vmap(hqk,khe->qhe)/dot_general | solution.py:65
  93.2 2.6 %copy.71 = f32[16,128,128]{2,0,1:T(8,128)} copy(f32[16,128,128]{1,2,0:T(8,128)} %convolution_bitcast_fusion.1) | data formatting | bytes 2097152
  95.8 1.7 multiply_reduce_fusion
  97.6 1.9 %fusion = bf16[16,128,264]{1,2,0:T(8,128)(2,1)S(1)} fusion(f32[16,128,264]{1,2,0:T(8,128)S(1)} %get-tuple-element.174, f32[16,128]{1,0:T(8,128)S(1)} %copy.72, f32[16,128]{1,0:T(8,128)S(1)} %log_add_fusion, bf16[1,8,16,128]{3,1,2,0:T(8,128)(2,1)S(1)} %bitcast.129, bf16[1,128,16,128]{3,1,2,0:T(8,128)(2,1)} %copy.53, bf16[1,128,16,128]{3,1,2,0:T(8,128)(2,1)} %bitcast.11, ...), kind=kOutput, calls=%fused_computation.3 | convolution fusion | flops 143818752 | bytes 4866048 | tf_op jit(solution)/shard_map/vmap(qhe,khe->hqk)/dot_general | solution.py:46
  99.6 0.7 multiply_bitcast_fusion
  100.3 1.0 fusion.3
  101.3 0.4 copy-done.2
  101.8 0.7 convolution_bitcast_fusion
  102.5 1.3 collective-permute-start.2
  103.9 35.6 %all_gather.16 = f32[8,8,16,128]{3,2,1,0:T(8,128)S(1)} all-gather(f32[1,8,16,128]{3,2,1,0:T(8,128)S(1)} %copy.56), channel_id=1, replica_groups=mesh['seq'=8,'head'=2,'dp'=2] {'seq'}, dimensions={0}, use_global_device_ids=true | all-gather | bytes 589824 | tf_op jit(solution)/shard_map/all_gather | solution.py:21
  139.5 31.6 %all_gather.17 = f32[8,8,16,128]{3,2,1,0:T(8,128)S(1)} all-gather(f32[1,8,16,128]{3,2,1,0:T(8,128)S(1)} %copy.58), channel_id=1, replica_groups=mesh['seq'=8,'head'=2,'dp'=2] {'seq'}, dimensions={0}, use_global_device_ids=true | all-gather | bytes 589824 | tf_op jit(solution)/shard_map/all_gather | solution.py:21
  171.1 0.4 while.18
  171.5 2.1 %fusion.4 = bf16[128,16,128]{2,0,1:T(8,128)(2,1)} fusion(f32[1,264,16,128]{3,1,2,0:T(8,128)} %copy-done.1), kind=kLoop, calls=%fused_computation.21 | loop fusion | bytes 1048576 | tf_op jit(solution)/shard_map/convert_element_type | solution.py:138
  173.7 1.3 collective-permute-start.3
  175.0 2.7 %fusion.2 = bf16[16,128,128]{2,1,0:T(8,128)(2,1)} fusion(bf16[16,128,264]{1,2,0:T(8,128)(2,1)S(1)} %copy-done.5, bf16[1,8,16,128]{3,1,2,0:T(8,128)(2,1)S(1)} %bitcast.127, bf16[1,128,16,128]{3,1,2,0:T(8,128)(2,1)} %copy.46, bf16[1,128,16,128]{3,1,2,0:T(8,128)(2,1)} %bitcast.5), kind=kOutput, calls=%fused_computation.12 | convolution fusion | flops 142180352 | bytes 2686976 | tf_op jit(solution)/shard_map/vmap(hqk,khe->qhe)/dot_general | solution.py:70
  177.6 2.0 %copy.63 = bf16[128,2048]{1,0:T(8,128)(2,1)} copy(bf16[128,2048]{0,1:T(8,128)(2,1)} %bitcast.125) | data formatting | bytes 1048576
  179.7 1.3 slice_add_fusion.1
  181.6 1.0 copy.64
  182.6 2.4 %collective-permute-done.3 = bf16[128,16,128]{2,0,1:T(8,128)(2,1)S(1)} collective-permute-done((bf16[128,16,128]{2,0,1:T(8,128)(2,1)}, bf16[128,16,128]{2,0,1:T(8,128)(2,1)S(1)}, u32[]{:S(2)}, u32[]{:S(2)}) %collective-permute-start.3) | collective-permute-done | bytes 524320 | tf_op jit(solution)/shard_map/ppermute | solution.py:14
  184.9 1.3 slice_add_fusion
  186.7 1.0 copy.65
  (58 shorter events, 3.3 us)
Async XLA Ops:
  0.6 86.7 %copy-start = (bf16[128,2048]{1,0:T(8,128)(2,1)S(1)}, bf16[128,2048]{1,0:T(8,128)(2,1)}, u32[]{:S(2)}) copy-start(bf16[128,2048]{1,0:T(8,128)(2,1)} %param.14) | copy-start | bytes 1572868
  0.6 7.4 %copy-start.6 = (bf16[128,2048]{1,0:T(8,128)(2,1)S(1)}, bf16[128,2048]{1,0:T(8,128)(2,1)}, u32[]{:S(2)}) copy-start(bf16[128,2048]{1,0:T(8,128)(2,1)} %param.16) | copy-start | bytes 1572868
  2.3 85.0 %collective-permute-start = (bf16[128,16,128]{2,0,1:T(8,128)(2,1)S(1)}, bf16[128,16,128]{2,0,1:T(8,128)(2,1)}, u32[]{:S(2)}, u32[]{:S(2)}) collective-permute-start(bf16[128,16,128]{2,0,1:T(8,128)(2,1)S(1)} %copy.42), channel_id=1, source_target_pairs={{0,4},{4,8},{8,12},{12,16},{16,20},{20,24},{24,28},{1,5},{5,9},{9,... | collective-permute-start | bytes 1572872 | tf_op jit(solution)/shard_map/ppermute | solution.py:14
  9.3 80.3 %collective-permute-start.1 = (bf16[128,16,128]{2,0,1:T(8,128)(2,1)}, bf16[128,16,128]{2,0,1:T(8,128)(2,1)}, u32[]{:S(2)}, u32[]{:S(2)}) collective-permute-start(bf16[128,16,128]{2,0,1:T(8,128)(2,1)} %copy.49), channel_id=1, source_target_pairs={{0,4},{4,8},{8,12},{12,16},{16,20},{20,24},{24,28},{1,5},{5,9},{9,... | collective-permute-start | bytes 1572872 | tf_op jit(solution)/shard_map/ppermute | solution.py:14
  13.0 73.3 %copy-start.3 = (bf16[128,2048]{1,0:T(8,128)(2,1)S(1)}, bf16[128,2048]{1,0:T(8,128)(2,1)}, u32[]{:S(2)}) copy-start(bf16[128,2048]{1,0:T(8,128)(2,1)} %param.17) | copy-start | bytes 1572868
  89.3 1.0 copy-start.7
  99.5 1.8 copy-start.4
  100.3 1.5 copy-start.2
  102.5 37.0 %copy-start.1 = (f32[1,264,16,128]{3,1,2,0:T(8,128)}, f32[1,264,16,128]{3,1,2,0:T(8,128)S(1)}, u32[]{:S(2)}) copy-start(f32[1,264,16,128]{3,1,2,0:T(8,128)S(1)} %convolution_bitcast_fusion) | copy-start | bytes 6488068
  102.5 77.2 %collective-permute-start.2 = (bf16[128,16,128]{2,0,1:T(8,128)(2,1)}, bf16[128,16,128]{2,0,1:T(8,128)(2,1)S(1)}, u32[]{:S(2)}, u32[]{:S(2)}) collective-permute-start(bf16[128,16,128]{2,0,1:T(8,128)(2,1)} %fusion.3), channel_id=1, source_target_pairs={{4,0},{8,4},{12,8},{16,12},{20,16},{24,20},{28,24},{5,1},{9,5},{13... | collective-permute-start | bytes 1572872 | tf_op jit(solution)/shard_map/ppermute | solution.py:14
  139.5 35.5 %copy-start.5 = (bf16[16,128,264]{1,2,0:T(8,128)(2,1)S(1)}, bf16[16,128,264]{1,2,0:T(8,128)(2,1)}, u32[]{:S(2)}) copy-start(bf16[16,128,264]{1,2,0:T(8,128)(2,1)} %copy-done.4) | copy-start | bytes 3244036
  173.7 11.3 %collective-permute-start.3 = (bf16[128,16,128]{2,0,1:T(8,128)(2,1)}, bf16[128,16,128]{2,0,1:T(8,128)(2,1)S(1)}, u32[]{:S(2)}, u32[]{:S(2)}) collective-permute-start(bf16[128,16,128]{2,0,1:T(8,128)(2,1)} %fusion.4), channel_id=1, source_target_pairs={{4,0},{8,4},{12,8},{16,12},{20,16},{24,20},{28,24},{5,1},{9,5},{13... | collective-permute-start | bytes 1572872 | tf_op jit(solution)/shard_map/ppermute | solution.py:14
where the time goes:
time: 188 us
  blocking collectives  138 us (73%)
  local copies, waits for them, and re-layouts  18.6 us (10%)
  starting transfers between devices  11.7 us (6%)
  matrix products  10.8 us (6%)
  other arithmetic  5.32 us (3%)
  waiting for transfers between devices  2.37 us (1%)
    all_gather x2, blocking collectives, prefix(): gathered = jax.tree.map(lambda a: lax.all_gather(a, axis), part)  67.2 us
    all_gather x1, blocking collectives, body(): lax.all_gather(strided_key, 'seq', axis=0, tiled=True)  40.1 us
    all_gather x1, blocking collectives, body(): lax.all_gather(strided_value, 'seq', axis=0, tiled=True)  30.4 us
    ppermute x4, starting transfers between devices, passed_along(): return lax.ppermute(block, axis, route)  11.7 us
    unnamed x23, local copies, waits for them, and re-layouts  10.4 us
  transfers between devices with their start and end apart: 4, of which 1 were waited for; matrix products, arithmetic and copies ran while one was open for 9% of the time, Pallas kernels for 0%

commit v1 on v0

--- a/solution.py
+++ b/solution.py
@@ -6,6 +6,22 @@
 E = 128
 B = 128
 masked_value = -1e30
+
+
+def ring_gather(x, axis, dim):
+    ways, here, step = (lax.axis_size(axis), lax.axis_index(axis), x.shape[dim])
+    shape = [n * ways if d == dim else n for d, n in enumerate(x.shape)]
+    full = lax.dynamic_update_slice_in_dim(jnp.zeros(shape, x.dtype), x, here * step, axis=dim)
+    going_up = going_down = x
+    for far in range(1, ways // 2 + 1):
+        going_up = lax.ppermute(going_up, axis, [(d, (d + 1) % ways) for d in range(ways)])
+        full = lax.dynamic_update_slice_in_dim(full, going_up, (here - far) % ways * step, axis=dim)
+        if 2 * far < ways:
+            going_down = lax.ppermute(going_down, axis, [(d, (d - 1) % ways) for d in range(ways)])
+            full = lax.dynamic_update_slice_in_dim(
+                full, going_down, (here + far) % ways * step, axis=dim
+            )
+    return full
 
 
 def passed_along(block, axis, distance):
@@ -95,7 +111,7 @@
     strided_value = value_blocks[:, B - 1]
     summary_key, summary_value = (
         lax.all_gather(strided_key, "seq", axis=0, tiled=True),
-        lax.all_gather(strided_value, "seq", axis=0, tiled=True),
+        ring_gather(strided_value, "seq", 0),
     )
     summary_count = summary_key.shape[0]
     key_before = jnp.concatenate([halo_key[None], key_blocks[:-1]], axis=0)

time: 188 us -> 182 us (0.968)
  blocking collectives: 138 us -> 102 us
  waiting for transfers between devices: 2.37 us -> 18.5 us
  starting transfers between devices: 11.7 us -> 24.6 us
    all_gather x1 -> x0, blocking collectives: 30.4 us -> none  [body(): lax.all_gather(strided_value, 'seq', axis=0, tiled=True)]
    ppermute x0 -> x7, waiting for transfers between devices: none -> 16.3 us  [the longest x4 16.3 us: ring_gather(): lax.ppermute(going_up, axis, [(d, (d + 1) % ways) for d in range(ways)])]
    ppermute x0 -> x7, starting transfers between devices: none -> 15.9 us  [the longest x3 10.4 us: ring_gather(): lax.ppermute(going_down, axis, [(d, (d - 1) % ways) for d in range(ways)])]
    all_gather x1, blocking collectives: 40.1 us -> 30.4 us  [body(): lax.all_gather(strided_key, 'seq', axis=0, tiled=True)]
    all_gather x2, blocking collectives: 67.2 us -> 71.3 us  [prefix(): gathered = jax.tree.map(lambda a: lax.all_gather(a, axis), part)]
    ppermute x4, starting transfers between devices: 11.7 us -> 8.67 us  [passed_along(): return lax.ppermute(block, axis, route)]
    unnamed x23 -> x28, local copies, waits for them, and re-layouts: 10.4 us -> 11.3 us
  transfers between devices with their start and end apart: 4 -> 11, of which waited for: 1 -> 3; matrix products, arithmetic and copies ran while one was open for 9% -> 9% of each run, Pallas kernels for 0% -> 0%
where the time goes in v1:
time: 182 us; the launch traced here: 181 us
  blocking collectives  102 us (56%)
  starting transfers between devices  24.6 us (14%)
  local copies, waits for them, and re-layouts  18.7 us (10%)
  waiting for transfers between devices  18.5 us (10%)
  matrix products  10.8 us (6%)
  other arithmetic  5.47 us (3%)
    all_gather x2, blocking collectives, prefix(): gathered = jax.tree.map(lambda a: lax.all_gather(a, axis), part)  71.3 us
    all_gather x1, blocking collectives, body(): lax.all_gather(strided_key, 'seq', axis=0, tiled=True)  30.4 us
    ppermute x4, waiting for transfers between devices, ring_gather(): lax.ppermute(going_up, axis, [(d, (d + 1) % ways) for d in range(ways)])  16.3 us
    unnamed x28, local copies, waits for them, and re-layouts  11.3 us
    ppermute x3, starting transfers between devices, ring_gather(): lax.ppermute(going_down, axis, [(d, (d - 1) % ways) for d in range(ways)])  10.4 us
    ppermute x4, starting transfers between devices, passed_along(): return lax.ppermute(block, axis, route)  8.67 us
    ppermute x4, starting transfers between devices, ring_gather(): lax.ppermute(going_up, axis, [(d, (d + 1) % ways) for d in range(ways)])  5.56 us
  transfers between devices with their start and end apart: 11, of which 3 were waited for; matrix products, arithmetic and copies ran while one was open for 9% of the time, Pallas kernels for 0%

profile of v1, /device:TPU:0, one launch (start us, length us, event | category | flops | bytes accessed | tf_op | source)
XLA Modules:
  0.0 181.2 jit_solution(17582025751792916397)
XLA Ops:
  0.7 1.4 copy.257
  2.4 3.0 %collective-permute-start.2 = (bf16[1,16,128]{2,1,0:T(8,128)(2,1)S(1)}, bf16[1,16,128]{2,1,0:T(8,128)(2,1)S(1)}, u32[]{:S(2)}, u32[]{:S(2)}) collective-permute-start(bf16[1,16,128]{2,1,0:T(8,128)(2,1)S(1)} %bitcast.141), channel_id=1, source_target_pairs={{0,4},{4,8},{8,12},{12,16},{16,20},{20,24},{24,28},{28,0},{1,5},{5... | collective-permute-start | bytes 12296 | tf_op jit(solution)/shard_map/ppermute | solution.py:17
  5.4 3.1 %collective-permute-start.3 = (bf16[1,16,128]{2,1,0:T(8,128)(2,1)S(1)}, bf16[1,16,128]{2,1,0:T(8,128)(2,1)S(1)}, u32[]{:S(2)}, u32[]{:S(2)}) collective-permute-start(bf16[1,16,128]{2,1,0:T(8,128)(2,1)S(1)} %bitcast.142), channel_id=1, source_target_pairs={{0,28},{4,0},{8,4},{12,8},{16,12},{20,16},{24,20},{28,24},{1,29},{... | collective-permute-start | bytes 12296 | tf_op jit(solution)/shard_map/ppermute | solution.py:20
  9.1 1.5 collective-permute-start
  10.6 1.0 copy.258
  11.6 4.6 %collective-permute-start.1 = (bf16[128,16,128]{2,0,1:T(8,128)(2,1)}, bf16[128,16,128]{2,0,1:T(8,128)(2,1)}, u32[]{:S(2)}, u32[]{:S(2)}) collective-permute-start(bf16[128,16,128]{2,0,1:T(8,128)(2,1)} %copy.258), channel_id=1, source_target_pairs={{0,4},{4,8},{8,12},{12,16},{16,20},{20,24},{24,28},{1,5},{5,9},{9,... | collective-permute-start | bytes 1572872 | tf_op jit(solution)/shard_map/ppermute | solution.py:30
  17.0 4.8 %collective-permute-start.5 = (bf16[1,16,128]{2,1,0:T(8,128)(2,1)S(1)}, bf16[1,16,128]{2,1,0:T(8,128)(2,1)S(1)}, u32[]{:S(2)}, u32[]{:S(2)}) collective-permute-start(bf16[1,16,128]{2,1,0:T(8,128)(2,1)S(1)} %collective-permute-done.3), channel_id=1, source_target_pairs={{0,28},{4,0},{8,4},{12,8},{16,12},{20,16},{24,20},{28,24},{1,29},{... | collective-permute-start | bytes 12296 | tf_op jit(solution)/shard_map/ppermute | solution.py:20
  21.7 11.4 %collective-permute-done.4 = bf16[1,16,128]{2,1,0:T(8,128)(2,1)S(1)} collective-permute-done((bf16[1,16,128]{2,1,0:T(8,128)(2,1)S(1)}, bf16[1,16,128]{2,1,0:T(8,128)(2,1)S(1)}, u32[]{:S(2)}, u32[]{:S(2)}) %collective-permute-start.4) | collective-permute-done | bytes 4128 | tf_op jit(solution)/shard_map/ppermute | solution.py:17
  33.2 2.5 %collective-permute-start.6 = (bf16[1,16,128]{2,1,0:T(8,128)(2,1)S(1)}, bf16[1,16,128]{2,1,0:T(8,128)(2,1)S(1)}, u32[]{:S(2)}, u32[]{:S(2)}) collective-permute-start(bf16[1,16,128]{2,1,0:T(8,128)(2,1)S(1)} %collective-permute-done.4), channel_id=1, source_target_pairs={{0,4},{4,8},{8,12},{12,16},{16,20},{20,24},{24,28},{28,0},{1,5},{5... | collective-permute-start | bytes 12296 | tf_op jit(solution)/shard_map/ppermute | solution.py:17
  35.6 30.4 %all-gather = bf16[8,1,16,128]{3,2,1,0:T(8,128)(2,1)S(1)} all-gather(bf16[1,1,16,128]{3,2,1,0:T(8,128)(2,1)S(1)} %copy.253), channel_id=2, replica_groups=mesh['seq'=8,'head'=2,'dp'=2] {'seq'}, dimensions={0}, use_global_device_ids=true | all-gather | bytes 36864 | tf_op jit(solution)/shard_map/all_gather | solution.py:113
  66.0 1.0 copy.255
  67.1 2.5 %collective-permute-start.7 = (bf16[1,16,128]{2,1,0:T(8,128)(2,1)S(1)}, bf16[1,16,128]{2,1,0:T(8,128)(2,1)S(1)}, u32[]{:S(2)}, u32[]{:S(2)}) collective-permute-start(bf16[1,16,128]{2,1,0:T(8,128)(2,1)S(1)} %collective-permute-done.5), channel_id=1, source_target_pairs={{0,28},{4,0},{8,4},{12,8},{16,12},{20,16},{24,20},{28,24},{1,29},{... | collective-permute-start | bytes 12296 | tf_op jit(solution)/shard_map/ppermute | solution.py:20
  69.6 0.9 copy.291
  71.0 4.9 %collective-permute-done.8 = bf16[1,16,128]{2,1,0:T(8,128)(2,1)S(1)} collective-permute-done((bf16[1,16,128]{2,1,0:T(8,128)(2,1)S(1)}, bf16[1,16,128]{2,1,0:T(8,128)(2,1)S(1)}, u32[]{:S(2)}, u32[]{:S(2)}) %collective-permute-start.8) | collective-permute-done | bytes 4128 | tf_op jit(solution)/shard_map/ppermute | solution.py:17
  76.8 1.9 %fusion.24 = (f32[16,128]{1,0:T(8,128)S(1)}, f32[16,128,264]{1,2,0:T(8,128)S(1)}) fusion(bf16[1,8,16,128]{3,1,2,0:T(8,128)(2,1)S(1)} %bitcast.132, bf16[1,128,16,128]{3,1,2,0:T(8,128)(2,1)} %copy.255, bf16[1,128,16,128]{3,1,2,0:T(8,128)(2,1)} %bitcast.143, pred[128,264]{0,1:T(8,128)(4,1)S(1)} %compare_select_fusion, bf16[128,2048]{1,0:T(8,128)(2,1)S(1)} %copy-done), kind=kOutput, calls=%fused_computation.55 | convolution fusion | flops 143276032 | bytes 3810304 | tf_op jit(solution)/shard_map/vmap(qhe,khe->hqk)/dot_general | solution.py:52
  79.7 2.8 %convolution_bitcast_fusion.1 = f32[16,128,128]{1,2,0:T(8,128)} fusion(bf16[1,8,16,128]{3,1,2,0:T(8,128)(2,1)S(1)} %dynamic_update_slice.39, bf16[1,128,16,128]{3,1,2,0:T(8,128)(2,1)S(1)} %copy-done.7, bf16[1,128,16,128]{3,1,2,0:T(8,128)(2,1)} %bitcast.11, f32[16,128,264]{1,2,0:T(8,128)S(1)} %get-tuple-element.237, f32[16,128]{1,0:T(8,128)S(1)} %log_add_fusion), kind=kOutput, calls=%fused_computation.11 | convolution fusion | flops 142737408 | bytes 4300800 | tf_op jit(solution)/shard_map/vmap(hqk,khe->qhe)/dot_general | solution.py:81
  82.5 2.6 %copy.286 = f32[16,128,128]{2,0,1:T(8,128)} copy(f32[16,128,128]{1,2,0:T(8,128)} %convolution_bitcast_fusion.1) | data formatting | bytes 2097152
  85.2 1.7 multiply_reduce_fusion
  86.9 1.9 %fusion = bf16[16,128,264]{1,2,0:T(8,128)(2,1)S(1)} fusion(f32[16,128,264]{1,2,0:T(8,128)S(1)} %get-tuple-element.237, f32[16,128]{1,0:T(8,128)S(1)} %copy.287, f32[16,128]{1,0:T(8,128)S(1)} %log_add_fusion, bf16[1,8,16,128]{3,1,2,0:T(8,128)(2,1)S(1)} %dynamic_update_slice.39, bf16[1,128,16,128]{3,1,2,0:T(8,128)(2,1)} %copy-done.6, ...), kind=kOutput, calls=%fused_computation.3 | convolution fusion | flops 143818752 | bytes 4866048 | tf_op jit(solution)/shard_map/vmap(qhe,khe->hqk)/dot_general | solution.py:62
  89.6 1.0 fusion.3
  91.9 1.3 collective-permute-start.9
  93.2 36.9 %all_gather.12 = f32[8,8,16,128]{3,2,1,0:T(8,128)S(1)} all-gather(f32[1,8,16,128]{3,2,1,0:T(8,128)S(1)} %copy.271), channel_id=1, replica_groups=mesh['seq'=8,'head'=2,'dp'=2] {'seq'}, dimensions={0}, use_global_device_ids=true | all-gather | bytes 589824 | tf_op jit(solution)/shard_map/all_gather | solution.py:37
  130.1 34.4 %all_gather.13 = f32[8,8,16,128]{3,2,1,0:T(8,128)S(1)} all-gather(f32[1,8,16,128]{3,2,1,0:T(8,128)S(1)} %copy.273), channel_id=1, replica_groups=mesh['seq'=8,'head'=2,'dp'=2] {'seq'}, dimensions={0}, use_global_device_ids=true | all-gather | bytes 589824 | tf_op jit(solution)/shard_map/all_gather | solution.py:37
  165.0 2.1 %fusion.4 = bf16[128,16,128]{2,0,1:T(8,128)(2,1)} fusion(f32[1,264,16,128]{3,1,2,0:T(8,128)} %copy-done.1), kind=kLoop, calls=%fused_computation.21 | loop fusion | bytes 1048576 | tf_op jit(solution)/shard_map/convert_element_type | solution.py:154
  167.1 1.3 collective-permute-start.10
  168.4 2.7 %fusion.2 = bf16[16,128,128]{2,1,0:T(8,128)(2,1)} fusion(bf16[16,128,264]{1,2,0:T(8,128)(2,1)S(1)} %copy-done.5, bf16[1,8,16,128]{3,1,2,0:T(8,128)(2,1)S(1)} %bitcast.133, bf16[1,128,16,128]{3,1,2,0:T(8,128)(2,1)} %copy.255, bf16[1,128,16,128]{3,1,2,0:T(8,128)(2,1)} %bitcast.144), kind=kOutput, calls=%fused_computation.12 | convolution fusion | flops 142180352 | bytes 2686976 | tf_op jit(solution)/shard_map/vmap(hqk,khe->qhe)/dot_general | solution.py:86
  171.1 2.0 %copy.278 = bf16[128,2048]{1,0:T(8,128)(2,1)} copy(bf16[128,2048]{0,1:T(8,128)(2,1)} %bitcast.131) | data formatting | bytes 1048576
  173.2 1.5 slice_add_fusion.1
  175.2 1.0 copy.279
  176.2 2.2 %collective-permute-done.10 = bf16[128,16,128]{2,0,1:T(8,128)(2,1)S(1)} collective-permute-done((bf16[128,16,128]{2,0,1:T(8,128)(2,1)}, bf16[128,16,128]{2,0,1:T(8,128)(2,1)S(1)}, u32[]{:S(2)}, u32[]{:S(2)}) %collective-permute-start.10) | collective-permute-done | bytes 524320 | tf_op jit(solution)/shard_map/ppermute | solution.py:30
  178.4 1.3 slice_add_fusion
  180.2 1.0 copy.280
  (90 shorter events, 7.4 us)
Async XLA Ops:
  0.6 76.1 %copy-start = (bf16[128,2048]{1,0:T(8,128)(2,1)S(1)}, bf16[128,2048]{1,0:T(8,128)(2,1)}, u32[]{:S(2)}) copy-start(bf16[128,2048]{1,0:T(8,128)(2,1)} %param.14) | copy-start | bytes 1572868
  0.6 7.9 %copy-start.8 = (bf16[128,2048]{1,0:T(8,128)(2,1)S(1)}, bf16[128,2048]{1,0:T(8,128)(2,1)}, u32[]{:S(2)}) copy-start(bf16[128,2048]{1,0:T(8,128)(2,1)} %param.15) | copy-start | bytes 1572868
  2.3 6.4 %copy-start.6 = (bf16[1,128,16,128]{3,1,2,0:T(8,128)(2,1)}, bf16[1,128,16,128]{3,1,2,0:T(8,128)(2,1)S(1)}, u32[]{:S(2)}) copy-start(bf16[1,128,16,128]{3,1,2,0:T(8,128)(2,1)S(1)} %copy.268) | copy-start | bytes 1572868
  2.4 13.9 %collective-permute-start.2 = (bf16[1,16,128]{2,1,0:T(8,128)(2,1)S(1)}, bf16[1,16,128]{2,1,0:T(8,128)(2,1)S(1)}, u32[]{:S(2)}, u32[]{:S(2)}) collective-permute-start(bf16[1,16,128]{2,1,0:T(8,128)(2,1)S(1)} %bitcast.141), channel_id=1, source_target_pairs={{0,4},{4,8},{8,12},{12,16},{16,20},{20,24},{24,28},{28,0},{1,5},{5... | collective-permute-start | bytes 12296 | tf_op jit(solution)/shard_map/ppermute | solution.py:17
  5.4 11.6 %collective-permute-start.3 = (bf16[1,16,128]{2,1,0:T(8,128)(2,1)S(1)}, bf16[1,16,128]{2,1,0:T(8,128)(2,1)S(1)}, u32[]{:S(2)}, u32[]{:S(2)}) collective-permute-start(bf16[1,16,128]{2,1,0:T(8,128)(2,1)S(1)} %bitcast.142), channel_id=1, source_target_pairs={{0,28},{4,0},{8,4},{12,8},{16,12},{20,16},{24,20},{28,24},{1,29},{... | collective-permute-start | bytes 12296 | tf_op jit(solution)/shard_map/ppermute | solution.py:20
  9.1 60.5 %copy-start.3 = (bf16[128,2048]{1,0:T(8,128)(2,1)S(1)}, bf16[128,2048]{1,0:T(8,128)(2,1)}, u32[]{:S(2)}) copy-start(bf16[128,2048]{1,0:T(8,128)(2,1)} %param.17) | copy-start | bytes 1572868
  9.1 66.8 %collective-permute-start = (bf16[128,16,128]{2,0,1:T(8,128)(2,1)S(1)}, bf16[128,16,128]{2,0,1:T(8,128)(2,1)S(1)}, u32[]{:S(2)}, u32[]{:S(2)}) collective-permute-start(bf16[128,16,128]{2,0,1:T(8,128)(2,1)S(1)} %copy.251), channel_id=1, source_target_pairs={{0,4},{4,8},{8,12},{12,16},{16,20},{20,24},{24,28},{1,5},{5,9},{9,... | collective-permute-start | bytes 1572872 | tf_op jit(solution)/shard_map/ppermute | solution.py:30
  11.6 67.5 %collective-permute-start.1 = (bf16[128,16,128]{2,0,1:T(8,128)(2,1)}, bf16[128,16,128]{2,0,1:T(8,128)(2,1)}, u32[]{:S(2)}, u32[]{:S(2)}) collective-permute-start(bf16[128,16,128]{2,0,1:T(8,128)(2,1)} %copy.258), channel_id=1, source_target_pairs={{0,4},{4,8},{8,12},{12,16},{16,20},{20,24},{24,28},{1,5},{5,9},{9,... | collective-permute-start | bytes 1572872 | tf_op jit(solution)/shard_map/ppermute | solution.py:30
  16.3 16.9 %collective-permute-start.4 = (bf16[1,16,128]{2,1,0:T(8,128)(2,1)S(1)}, bf16[1,16,128]{2,1,0:T(8,128)(2,1)S(1)}, u32[]{:S(2)}, u32[]{:S(2)}) collective-permute-start(bf16[1,16,128]{2,1,0:T(8,128)(2,1)S(1)} %collective-permute-done.2), channel_id=1, source_target_pairs={{0,4},{4,8},{8,12},{12,16},{16,20},{20,24},{24,28},{28,0},{1,5},{5... | collective-permute-start | bytes 12296 | tf_op jit(solution)/shard_map/ppermute | solution.py:17
  17.0 50.1 %collective-permute-start.5 = (bf16[1,16,128]{2,1,0:T(8,128)(2,1)S(1)}, bf16[1,16,128]{2,1,0:T(8,128)(2,1)S(1)}, u32[]{:S(2)}, u32[]{:S(2)}) collective-permute-start(bf16[1,16,128]{2,1,0:T(8,128)(2,1)S(1)} %collective-permute-done.3), channel_id=1, source_target_pairs={{0,28},{4,0},{8,4},{12,8},{16,12},{20,16},{24,20},{28,24},{1,29},{... | collective-permute-start | bytes 12296 | tf_op jit(solution)/shard_map/ppermute | solution.py:20
  33.2 36.4 %collective-permute-start.6 = (bf16[1,16,128]{2,1,0:T(8,128)(2,1)S(1)}, bf16[1,16,128]{2,1,0:T(8,128)(2,1)S(1)}, u32[]{:S(2)}, u32[]{:S(2)}) collective-permute-start(bf16[1,16,128]{2,1,0:T(8,128)(2,1)S(1)} %collective-permute-done.4), channel_id=1, source_target_pairs={{0,4},{4,8},{8,12},{12,16},{16,20},{20,24},{24,28},{28,0},{1,5},{5... | collective-permute-start | bytes 12296 | tf_op jit(solution)/shard_map/ppermute | solution.py:17
  67.1 3.8 %collective-permute-start.7 = (bf16[1,16,128]{2,1,0:T(8,128)(2,1)S(1)}, bf16[1,16,128]{2,1,0:T(8,128)(2,1)S(1)}, u32[]{:S(2)}, u32[]{:S(2)}) collective-permute-start(bf16[1,16,128]{2,1,0:T(8,128)(2,1)S(1)} %collective-permute-done.5), channel_id=1, source_target_pairs={{0,28},{4,0},{8,4},{12,8},{16,12},{20,16},{24,20},{28,24},{1,29},{... | collective-permute-start | bytes 12296 | tf_op jit(solution)/shard_map/ppermute | solution.py:20
  69.6 6.3 %collective-permute-start.8 = (bf16[1,16,128]{2,1,0:T(8,128)(2,1)S(1)}, bf16[1,16,128]{2,1,0:T(8,128)(2,1)S(1)}, u32[]{:S(2)}, u32[]{:S(2)}) collective-permute-start(bf16[1,16,128]{2,1,0:T(8,128)(2,1)S(1)} %collective-permute-done.6), channel_id=1, source_target_pairs={{0,4},{4,8},{8,12},{12,16},{16,20},{20,24},{24,28},{28,0},{1,5},{5... | collective-permute-start | bytes 12296 | tf_op jit(solution)/shard_map/ppermute | solution.py:17
  76.0 0.8 copy-start.9
  78.7 1.0 copy-start.7
  88.9 1.8 copy-start.4
  89.6 1.5 copy-start.2
  91.9 38.2 %copy-start.1 = (f32[1,264,16,128]{3,1,2,0:T(8,128)}, f32[1,264,16,128]{3,1,2,0:T(8,128)S(1)}, u32[]{:S(2)}) copy-start(f32[1,264,16,128]{3,1,2,0:T(8,128)S(1)} %convolution_bitcast_fusion) | copy-start | bytes 6488068
  91.9 81.3 %collective-permute-start.9 = (bf16[128,16,128]{2,0,1:T(8,128)(2,1)}, bf16[128,16,128]{2,0,1:T(8,128)(2,1)}, u32[]{:S(2)}, u32[]{:S(2)}) collective-permute-start(bf16[128,16,128]{2,0,1:T(8,128)(2,1)} %fusion.3), channel_id=1, source_target_pairs={{4,0},{8,4},{12,8},{16,12},{20,16},{24,20},{28,24},{5,1},{9,5},{13... | collective-permute-start | bytes 1572872 | tf_op jit(solution)/shard_map/ppermute | solution.py:30
  130.1 38.3 %copy-start.5 = (bf16[16,128,264]{1,2,0:T(8,128)(2,1)S(1)}, bf16[16,128,264]{1,2,0:T(8,128)(2,1)}, u32[]{:S(2)}) copy-start(bf16[16,128,264]{1,2,0:T(8,128)(2,1)} %copy-done.4) | copy-start | bytes 3244036
  167.1 11.3 %collective-permute-start.10 = (bf16[128,16,128]{2,0,1:T(8,128)(2,1)}, bf16[128,16,128]{2,0,1:T(8,128)(2,1)S(1)}, u32[]{:S(2)}, u32[]{:S(2)}) collective-permute-start(bf16[128,16,128]{2,0,1:T(8,128)(2,1)} %fusion.4), channel_id=1, source_target_pairs={{4,0},{8,4},{12,8},{16,12},{20,16},{24,20},{28,24},{5,1},{9,5},{13... | collective-permute-start | bytes 1572872 | tf_op jit(solution)/shard_map/ppermute | solution.py:30
